TPU v7x, 32 devices: a whole 2x2x4 slice. The times are simulated.
32 devices in a mesh: gx: 4 (over z), gy: 2 (over x), gz: 4 (over y, core).
Axes of the slice: x: 2, y: 2, z: 4, core: 2. Of those that a mesh axis runs over, the one named last changes fastest.
Arguments:
- weights: bfloat16 [32, 32, 32, 2, 8, 512], P('gx', 'gy', 'gz'), may hold values from -6 to 6
- angles: float32 [3, 32, 32, 32, 512], P(None, 'gx', 'gy', 'gz'), may hold values from -3.140625 to 3.140625
- translation: bfloat16 [8, 512, 512], replicated, may hold values from -0.09375 to 0.09375
Outputs:
- transformed: bfloat16 [32, 32, 32, 2, 8, 512], P('gx', 'gy', 'gz')
All inputs are finite; a program needn't handle non-finite values.
Results may differ from a plain program's by a relative error of at most 0.025.
Values may be sent and summed in bfloat16 or wider, within the bound.
A program may use at most 128 MiB of HBM per device.

v0:
```python
import jax
import jax.numpy as jnp
from jax import lax
from jax.sharding import PartitionSpec as P

PX = 32
PY = 32
PZ = 32
LEVELS = 3


def rotate_blocks(current, angle):
    real_part = current[:, :, :, 0].astype(jnp.float32)
    imag_part = current[:, :, :, 1].astype(jnp.float32)
    cosine = jnp.cos(angle)[:, :, :, :, None, :]
    sine = jnp.sin(angle)[:, :, :, :, None, :]
    rotated_re = real_part * cosine - imag_part * sine
    rotated_im = real_part * sine + imag_part * cosine
    return jnp.stack([rotated_re, rotated_im], axis=3).astype(jnp.bfloat16)


def fold_local(child_terms, dim_pos, low_span):
    dims_shape = child_terms.shape
    count = dims_shape[dim_pos]
    split = child_terms.reshape(
        dims_shape[:dim_pos] + (count // (2 * low_span), 2, low_span) + dims_shape[dim_pos + 1 :]
    )
    first = jnp.take(split, 0, axis=dim_pos + 1).astype(jnp.float32)
    second = jnp.take(split, 1, axis=dim_pos + 1).astype(jnp.float32)
    added = (first + second).astype(jnp.bfloat16)
    return added.reshape(dims_shape[:dim_pos] + (count // 2,) + dims_shape[dim_pos + 1 :])


def insert_bit(lower, upper, dim_pos, low_span):
    dims_shape = lower.shape
    count = dims_shape[dim_pos]
    inner_shape = dims_shape[:dim_pos] + (count // low_span, low_span) + dims_shape[dim_pos + 1 :]
    stacked = jnp.stack([lower.reshape(inner_shape), upper.reshape(inner_shape)], axis=dim_pos + 1)
    return stacked.reshape(dims_shape[:dim_pos] + (2 * count,) + dims_shape[dim_pos + 1 :])


def translate_all(summed, translation, local_dims, chosen_bits):
    if not local_dims:
        orient = 4 * chosen_bits[0] + 2 * chosen_bits[1] + chosen_bits[2]
        matrix = lax.dynamic_index_in_dim(translation, orient, 0, keepdims=False)
        rows = summed.reshape(-1, summed.shape[-1])
        result = jnp.dot(rows, matrix, preferred_element_type=jnp.float32)
        return result.astype(jnp.bfloat16).reshape(summed.shape)
    dim_pos, low_span = local_dims[0]
    halves = []
    for t in (0, 1):
        picked = dict(chosen_bits)
        picked[dim_pos] = t
        halves.append(translate_all(summed, translation, local_dims[1:], picked))
    return insert_bit(halves[0], halves[1], dim_pos, low_span)


def levels_moved(weights, angles, translation):
    count_x = lax.axis_size("gx")
    count_y = lax.axis_size("gy")
    count_z = lax.axis_size("gz")
    count_yz = count_y * count_z
    devices_all = count_x * count_yz
    top_range = 2**LEVELS
    low_x = PX // top_range
    low_y = PY // top_range
    low_z = PZ // top_range
    high_x = top_range // count_x
    high_y = top_range // count_y
    high_z = top_range // count_z
    local_x, local_y, local_z = (weights.shape[0], weights.shape[1], weights.shape[2])
    rhs_width = weights.shape[4]
    cheb_width = weights.shape[5]
    block_count = low_x * low_y * low_z
    item_share = block_count * rhs_width // devices_all
    repeat_count = max(1, devices_all // block_count)
    block_share = max(1, block_count // devices_all)
    rhs_share = item_share // block_share
    sectioned = weights.reshape(
        high_x, low_x, high_y, low_y, high_z, low_z, 2, rhs_width, cheb_width
    )
    sectioned = sectioned.transpose(0, 2, 4, 6, 1, 3, 5, 7, 8)
    sectioned = sectioned.reshape(
        1, 1, high_x, high_y, high_z, 2, count_x, block_count * rhs_width // count_x, cheb_width
    )
    arrived = lax.all_to_all(
        lax.all_to_all(sectioned, "gx", split_axis=6, concat_axis=0, tiled=True),
        ("gy", "gz"),
        split_axis=7,
        concat_axis=1,
        tiled=True,
    )
    current = arrived.reshape(
        count_x, count_y, count_z, high_x, high_y, high_z, 2, block_share, rhs_share, cheb_width
    )
    current = current.transpose(0, 3, 1, 4, 2, 5, 6, 7, 8, 9)
    current = current.reshape(
        top_range, top_range, top_range, 2, block_share, rhs_share, cheb_width
    )
    phase_local = angles.reshape(LEVELS, high_x, low_x, high_y, low_y, high_z, low_z, cheb_width)
    phase_local = phase_local.transpose(1, 3, 5, 0, 2, 4, 6, 7)
    phase_local = phase_local.reshape(
        1, 1, high_x, high_y, high_z, LEVELS, block_count, 1, cheb_width
    )
    phase_local = jnp.broadcast_to(
        phase_local, (1, 1, high_x, high_y, high_z, LEVELS, block_count, repeat_count, cheb_width)
    )
    phase_local = phase_local.reshape(
        1,
        1,
        high_x,
        high_y,
        high_z,
        LEVELS,
        count_x,
        block_count * repeat_count // count_x,
        cheb_width,
    )
    phase_in = lax.all_to_all(
        lax.all_to_all(phase_local, "gx", split_axis=6, concat_axis=0, tiled=True),
        ("gy", "gz"),
        split_axis=7,
        concat_axis=1,
        tiled=True,
    )
    phase_all = phase_in.reshape(
        count_x, count_y, count_z, high_x, high_y, high_z, LEVELS, block_share, cheb_width
    )
    phase_all = phase_all.transpose(6, 0, 3, 1, 4, 2, 5, 7, 8)
    phase_all = phase_all.reshape(LEVELS, top_range, top_range, top_range, block_share, cheb_width)
    for level_idx in range(LEVELS):
        child_terms = rotate_blocks(current, phase_all[level_idx])
        local_dims = []
        for d in range(3):
            low_span = 2 ** (LEVELS - 1 - level_idx)
            child_terms = fold_local(child_terms, d, low_span)
            local_dims.append((d, low_span))
        current = translate_all(child_terms, translation, local_dims, dict())
    leaving = current.reshape(
        count_x, high_x, count_y, high_y, count_z, high_z, 2, item_share, cheb_width
    )
    leaving = leaving.transpose(0, 2, 4, 1, 3, 5, 6, 7, 8)
    leaving = leaving.reshape(
        count_x, count_yz, high_x, high_y, high_z, 2, 1, item_share, cheb_width
    )
    returned = lax.all_to_all(
        lax.all_to_all(leaving, "gx", split_axis=0, concat_axis=6, tiled=True),
        ("gy", "gz"),
        split_axis=1,
        concat_axis=7,
        tiled=True,
    )
    result = returned.reshape(high_x, high_y, high_z, 2, low_x, low_y, low_z, rhs_width, cheb_width)
    result = result.transpose(0, 4, 1, 5, 2, 6, 3, 7, 8)
    return result.reshape(local_x, local_y, local_z, 2, rhs_width, cheb_width)


def shards(weights, angles, translation):
    return levels_moved(weights, angles, translation)


def solution(mesh):
    in_specs = (P("gx", "gy", "gz", None, None, None), P(None, "gx", "gy", "gz", None), P())
    out_specs = P("gx", "gy", "gz", None, None, None)
    return jax.shard_map(shards, mesh=mesh, in_specs=in_specs, out_specs=out_specs, check_vma=False)
```

profile of v0, /device:TPU:0, one launch (start us, length us, event | category | flops | bytes accessed | tf_op | source)
XLA Modules:
  0.0 1646.1 jit_solution(8056960758085510483)
XLA Ops:
  0.0 7.4 reshape.186
  7.4 7.2 copy.347
  14.6 4.6 copy.348
  19.2 6.3 all-to-all-start.2
  25.5 8.7 copy.341
  34.2 6.9 copy.342
  41.1 123.2 %all-to-all-done.2 = f32[1,1,2,4,2,3,4,16,512]{8,7,5,4,3,2,1,0,6:T(8,128)} async-done(((f32[1,1,2,4,2,3,4,16,512]{8,7,5,4,3,2,1,0,6:T(8,128)}), f32[1,1,2,4,2,3,4,16,512]{8,7,5,4,3,2,1,0,6:T(8,128)}, u32[]{:S(2)}, u32[]{:S(2)}) %all-to-all-start.2) | async-done | bytes 6291488 | tf_op jit(solution)/shard_map/all_to_all | solution.py:120
  164.3 7.5 all-to-all-start
  171.8 9.5 copy.349
  181.2 353.1 %all-to-all-done = bf16[1,1,2,4,2,2,4,128,512]{8,7,5,4,3,2,1,0,6:T(8,128)(2,1)} async-done(((bf16[1,1,2,4,2,2,4,128,512]{8,7,5,4,3,2,1,0,6:T(8,128)(2,1)}), bf16[1,1,2,4,2,2,4,128,512]{8,7,5,4,3,2,1,0,6:T(8,128)(2,1)}, u32[]{:S(2)}, u32[]{:S(2)}) %all-to-all-start) | async-done | bytes 16777248 | tf_op jit(solution)/shard_map/all_to_all | solution.py:87
  534.3 4.8 all-to-all-start.3
  539.1 22.0 %copy.343 = bf16[4,1,2,4,2,2,1,128,512]{8,0,5,4,3,2,6,1,7:T(4,128)(2,1)} copy(bf16[4,1,2,4,2,2,1,128,512]{8,7,5,4,3,2,0,6,1:T(8,128)(2,1)} %bitcast.5) | data formatting | bytes 33554432 | tf_op jit(solution)/shard_map/all_to_all | solution.py:87
  561.1 48.6 %all-to-all-done.3 = f32[4,1,2,4,2,3,1,16,512]{8,0,5,4,3,2,6,1,7:T(4,128)} async-done(((f32[4,1,2,4,2,3,1,16,512]{8,0,5,4,3,2,6,1,7:T(4,128)}), f32[4,1,2,4,2,3,1,16,512]{8,0,5,4,3,2,6,1,7:T(4,128)}, u32[]{:S(2)}, u32[]{:S(2)}) %all-to-all-start.3) | async-done | bytes 6291488 | tf_op jit(solution)/shard_map/all_to_all | solution.py:119
  609.7 5.9 all-to-all-start.1
  615.7 7.6 copy.350
  623.3 4.0 copy.432
  627.4 44.0 %slice_cosine_fusion.2 = (f32[1,4,2,2,4,4,2,2,512]{8,5,7,6,4,3,2,1,0:T(4,128)S(1)}, f32[1,4,2,2,4,4,2,2,512]{8,5,7,6,4,3,2,1,0:T(4,128)S(1)}, f32[1,4,2,2,4,4,2,...) fusion(f32[3,4,2,2,4,4,2,2,512]{8,5,7,6,4,3,2,1,0:T(4,128)S(1)}, ...), kind=kLoop, calls=%fused_computation.116 | loop fusion | bytes 18874368 | tf_op jit(solution)/shard_map/cos | solution.py:15
  686.0 112.7 %all-to-all-done.1 = bf16[4,1,2,4,2,2,1,128,512]{8,0,5,4,3,2,6,1,7:T(4,128)(2,1)} async-done(((bf16[4,1,2,4,2,2,1,128,512]{8,0,5,4,3,2,6,1,7:T(4,128)(2,1)}), bf16[4,1,2,4,2,2,1,128,512]{8,0,5,4,3,2,6,1,7:T(4,128)(2,1)}, u32[]{:S(2)}, u32[]{:S(2)}) %all-to-all-start.1) | async-done | bytes 16777248 | tf_op jit(solution)/shard_map/all_to_all | solution.py:86
  798.7 15.5 copy.344
  817.1 9.0 fusion.3
  826.1 7.0 add_convert_fusion.2
  854.6 6.3 pad_maximum_fusion.6
  860.9 8.5 copy.367
  874.7 6.6 pad_maximum_fusion.5
  881.2 8.5 copy.362
  889.8 8.0 pad_maximum_fusion
  897.8 9.1 fusion.7
  906.9 8.9 add_convert_fusion.1
  915.8 8.3 copy.373
  924.0 4.4 add_convert_fusion.4
  947.5 6.3 pad_maximum_fusion.8
  953.8 8.5 copy.385
  967.5 6.8 pad_maximum_fusion.7
  974.3 8.5 copy.380
  982.9 8.0 pad_maximum_fusion.1
  993.7 9.0 fusion.9
  1002.8 4.6 fusion.12
  1007.4 4.0 add_convert_fusion
  1032.8 6.3 pad_maximum_fusion.10
  1039.1 8.5 copy.402
  1052.9 6.3 pad_maximum_fusion.9
  1059.2 8.5 copy.397
  1067.8 8.0 maximum_bitcast_fusion
  1075.8 3.0 copy.403
  1078.7 365.9 %all_to_all.99 = bf16[4,8,2,4,2,2,1,16,512]{8,7,5,4,3,2,1,6,0:T(8,128)(2,1)S(1)} all-to-all(bf16[4,8,2,4,2,2,1,16,512]{8,7,5,4,3,2,1,6,0:T(8,128)(2,1)S(1)} %bitcast.350), channel_id=1, replica_groups=mesh['gx'=4,'gy'=2,'gz'=4] {'gx'}, dimensions={0} | all-to-all | bytes 33554432 | tf_op jit(solution)/shard_map/all_to_all | solution.py:147
  1447.1 188.2 %all_to_all.100 = bf16[1,8,2,4,2,2,4,16,512]{8,7,5,4,3,2,6,0,1:T(8,128)(2,1)S(1)} all-to-all(bf16[1,8,2,4,2,2,4,16,512]{8,7,5,4,3,2,6,0,1:T(8,128)(2,1)S(1)} %copy.405), channel_id=1, replica_groups=mesh['gx'=4,'gy'=2,'gz'=4] {'gy','gz'}, dimensions={1} | all-to-all | bytes 33554432 | tf_op jit(solution)/shard_map/all_to_all | solution.py:146
  1635.2 3.6 copy.406
  1638.9 7.1 copy.407
  (62 shorter events, 99.9 us)
Async XLA Ops:
  19.2 145.1 %all-to-all-start.2 = ((f32[1,1,2,4,2,3,4,16,512]{8,7,5,4,3,2,1,0,6:T(8,128)}), f32[1,1,2,4,2,3,4,16,512]{8,7,5,4,3,2,1,0,6:T(8,128)}, u32[]{:S(2)}, u32[]{:S(2)}) async-start(f32[1,1,2,4,2,3,4,16,512]{8,7,5,4,3,2,1,0,6:T(8,128)} %copy.348), calls=%async_computation.2 | async-start | bytes 12582912 | tf_op jit(solution)/shard_map/all_to_all | solution.py:120
  164.3 370.0 %all-to-all-start = ((bf16[1,1,2,4,2,2,4,128,512]{8,7,5,4,3,2,1,0,6:T(8,128)(2,1)}), bf16[1,1,2,4,2,2,4,128,512]{8,7,5,4,3,2,1,0,6:T(8,128)(2,1)}, u32[]{:S(2)}, u32[]{:S(2)}) async-start(bf16[1,1,2,4,2,2,4,128,512]{8,7,5,4,3,2,1,0,6:T(8,128)(2,1)} %copy.342), calls=%async_computation | async-start | bytes 33554432 | tf_op jit(solution)/shard_map/all_to_all | solution.py:87
  534.3 75.4 %all-to-all-start.3 = ((f32[4,1,2,4,2,3,1,16,512]{8,0,5,4,3,2,6,1,7:T(4,128)}), f32[4,1,2,4,2,3,1,16,512]{8,0,5,4,3,2,6,1,7:T(4,128)}, u32[]{:S(2)}, u32[]{:S(2)}) async-start(f32[4,1,2,4,2,3,1,16,512]{8,0,5,4,3,2,6,1,7:T(4,128)} %copy.349), calls=%async_computation.3 | async-start | bytes 12582912 | tf_op jit(solution)/shard_map/all_to_all | solution.py:119
  609.7 188.9 %all-to-all-start.1 = ((bf16[4,1,2,4,2,2,1,128,512]{8,0,5,4,3,2,6,1,7:T(4,128)(2,1)}), bf16[4,1,2,4,2,2,1,128,512]{8,0,5,4,3,2,6,1,7:T(4,128)(2,1)}, u32[]{:S(2)}, u32[]{:S(2)}) async-start(bf16[4,1,2,4,2,2,1,128,512]{8,0,5,4,3,2,6,1,7:T(4,128)(2,1)} %copy.343), calls=%async_computation.1 | async-start | bytes 33554432 | tf_op jit(solution)/shard_map/all_to_all | solution.py:86
  835.6 2.2 copy-start.3
  869.5 2.9 copy-start
  928.5 2.2 copy-start.4
  962.3 2.9 copy-start.1
  1013.8 2.2 copy-start.5
  1047.7 2.9 copy-start.2
where the time goes:
time: 1650 us
  waiting for transfers between devices  638 us (39%)
  blocking collectives  554 us (34%)
  local copies, waits for them, and re-layouts  237 us (14%)
  other arithmetic  151 us (9%)
  matrix products  42.2 us (3%)
  starting transfers between devices  24.5 us (1%)
    all_to_all x1, blocking collectives, levels_moved(): lax.all_to_all(leaving, 'gx', split_axis=0, concat_axis=6, tiled=True)  366 us
    all_to_all x1, waiting for transfers between devices, levels_moved(): lax.all_to_all(sectioned, 'gx', split_axis=6, concat_axis=0, tiled=True)  353 us
    all_to_all x1, blocking collectives, levels_moved(): lax.all_to_all(lax.all_to_all(leaving, 'gx', split_axis=0, concat_axis=6,...  188 us
    all_to_all x1, waiting for transfers between devices, levels_moved(): lax.all_to_all(phase_local, 'gx', split_axis=6, concat_axis=0, tiled=True)  123 us
    all_to_all x1, waiting for transfers between devices, levels_moved(): lax.all_to_all(lax.all_to_all(sectioned, 'gx', split_axis=6, concat_axis=...  113 us
    another operation x20, other arithmetic, insert_bit(): jnp.stack([lower.reshape(inner_shape), upper.reshape(inner_shape)], axis=...  78.2 us
    another operation x7, local copies, waits for them, and re-layouts, insert_bit(): jnp.stack([lower.reshape(inner_shape), upper.reshape(inner_shape)], axis=...  54.1 us
    cos x4, local copies, waits for them, and re-layouts, rotate_blocks(): cosine = jnp.cos(angle)[:, :, :, :, None, :]  51.3 us
  transfers between devices with their start and end apart: 4, of which 4 were waited for; matrix products, arithmetic and copies ran while one was open for 7% of the time, Pallas kernels for 0%

commit v1 on v0

v1 whole, which is shorter than its diff:
```python
import jax
import jax.numpy as jnp
from jax import lax
from jax.experimental import pallas as pl
from jax.experimental.pallas import tpu as pltpu
from jax.sharding import PartitionSpec as P

LEVELS = 3
AXES = ("gx", "gy", "gz")


def sincos(angle):
    half = angle * 0.5
    sq = half * half
    sin_half = -1.0 / 39916800.0
    for c in (1.0 / 362880.0, -1.0 / 5040.0, 1.0 / 120.0, -1.0 / 6.0, 1.0):
        sin_half = sin_half * sq + c
    sin_half = sin_half * half
    cos_half = 1.0 / 479001600.0
    for c in (-1.0 / 3628800.0, 1.0 / 40320.0, -1.0 / 720.0, 1.0 / 24.0, -0.5, 1.0):
        cos_half = cos_half * sq + c
    return 1.0 - 2.0 * sin_half * sin_half, 2.0 * sin_half * cos_half


def halve_sum(terms, axis_name, dim):
    count = lax.axis_size(axis_name)
    bit = lax.axis_index(axis_name) // (count // 2)
    mine = lax.dynamic_index_in_dim(terms, bit, dim, keepdims=True)
    theirs = lax.dynamic_index_in_dim(terms, 1 - bit, dim, keepdims=True)
    pairs = [(i, (i + count // 2) % count) for i in range(count)]
    got = lax.ppermute(theirs, axis_name, pairs)
    return (mine.astype(jnp.float32) + got.astype(jnp.float32)).astype(jnp.bfloat16)


def exchange_low(terms, axis_name, dim):
    count = lax.axis_size(axis_name)
    low = count // 2
    if low == 1:
        return terms
    groups = [[h * low + i for i in range(low)] for h in range(2)]
    return lax.all_to_all(
        terms, axis_name, split_axis=dim, concat_axis=dim, axis_index_groups=groups, tiled=True
    )


def rotate_sum(current, angle):
    cosine, sine = sincos(angle.astype(jnp.float32))
    cosine = cosine[..., None, :]
    sine = sine[..., None, :]
    re = current[0].astype(jnp.float32)
    im = current[1].astype(jnp.float32)
    return re * cosine - im * sine, re * sine + im * cosine


def shards(weights, angles, translation):
    counts = [lax.axis_size(a) for a in AXES]
    count_x, count_y, count_z = counts
    devices = count_x * count_y * count_z
    count_yz = count_y * count_z
    top = 2**LEVELS
    hx, hy, hz = (top // c for c in counts)
    lx, ly, lz = (weights.shape[0] // hx, weights.shape[1] // hy, weights.shape[2] // hz)
    rhs, cheb = weights.shape[4], weights.shape[5]
    blocks = lx * ly * lz
    share = blocks * rhs // devices
    block_share = max(1, blocks // devices)
    rhs_share = share // block_share
    repeat = max(1, devices // blocks)
    C = hx * hy * hz

    ph = angles[1:].astype(jnp.bfloat16)
    ph = ph.reshape(LEVELS - 1, hx, lx, hy, ly, hz, lz, cheb).transpose(1, 3, 5, 0, 2, 4, 6, 7)
    ph = ph.reshape(1, 1, hx, hy, hz, LEVELS - 1, blocks, 1, cheb)
    ph = jnp.broadcast_to(ph, ph.shape[:7] + (repeat, cheb))
    ph = ph.reshape(
        1, 1, hx, hy, hz, LEVELS - 1, count_x, blocks * repeat // count_x, cheb
    )
    ph = lax.all_to_all(ph, "gx", split_axis=6, concat_axis=0, tiled=True)
    ph = lax.all_to_all(ph, ("gy", "gz"), split_axis=7, concat_axis=1, tiled=True)
    ph = ph.reshape(count_x, count_y, count_z, hx, hy, hz, LEVELS - 1, block_share, cheb)
    ph = ph.transpose(6, 0, 3, 1, 4, 2, 5, 7, 8)
    ph = ph.reshape(LEVELS - 1, top, top, top, block_share, cheb)

    parts = [
        v.reshape(C, 2, count_x // 2, 2, count_y // 2, 2, count_z // 2, share, cheb)
        for v in first_rotate(weights, angles[0], (lx, ly, lz))
    ]
    where = {"gx": 1, "gy": 3, "gz": 5}
    orders = [("gx", "gy", "gz"), ("gy", "gz", "gx"), ("gz", "gx", "gy")]
    cuts = [C * i // 3 for i in range(4)]
    streams = {}
    for p in range(2):
        for k in range(3):
            if cuts[k + 1] > cuts[k]:
                streams[p, k] = parts[p][cuts[k] : cuts[k + 1]]
    for step in range(3):
        for p, k in list(streams):
            name = orders[k][step]
            streams[p, k] = halve_sum(streams[p, k], name, where[name])
    both = jnp.stack(
        [jnp.concatenate([streams[p, k] for k in range(3) if (p, k) in streams]) for p in range(2)]
    )
    both = both.reshape(2, C, count_x // 2, count_y // 2, count_z // 2, share, cheb)
    for dim, name in ((2, "gx"), (3, "gy"), (4, "gz")):
        both = exchange_low(both, name, dim)
    both = both.reshape(
        2, hx, hy, hz, count_x // 2, count_y // 2, count_z // 2, block_share, rhs_share, cheb
    )
    summed = both.transpose(0, 4, 1, 5, 2, 6, 3, 7, 8, 9)
    q = top // 2
    summed = summed.reshape(2, q * q * q * share, cheb)

    def translate(s):
        return jnp.einsum(
            "crk,tkn->ctrn", s, translation, preferred_element_type=jnp.float32
        ).astype(jnp.bfloat16)

    tail = (block_share, rhs_share, cheb)
    w = translate(summed)
    w = w.reshape((2, 2, 2, 2, 2, 2, 2, 2, 2, 2) + tail)
    ang = ph[0].reshape((2,) * 9 + (block_share, cheb))
    ang = ang.transpose(0, 3, 6, 1, 2, 4, 5, 7, 8, 9, 10)
    r, i = rotate_sum(w, ang)
    summed = jnp.stack([r.sum((3, 5, 7)), i.sum((3, 5, 7))]).astype(jnp.bfloat16)
    w = translate(summed.reshape(2, q * q * q * share, cheb))
    w = w.reshape((2,) + (2,) * 9 + tail)
    ang = ph[1].reshape((2,) * 9 + (block_share, cheb))
    ang = ang.transpose(1, 4, 7, 0, 3, 6, 2, 5, 8, 9, 10)
    r, i = rotate_sum(w, ang)
    summed = jnp.stack([r.sum((6, 7, 8)), i.sum((6, 7, 8))]).astype(jnp.bfloat16)
    summed = summed.transpose(4, 1, 5, 2, 6, 3, 0, 7, 8, 9)
    summed = summed.reshape(q, q, q, 2, share, cheb)
    keep = []
    for d, c in enumerate(counts):
        if c > q:
            summed = jnp.repeat(summed, c // q, axis=d)
        keep.append(max(1, q // c))
    kx, ky, kz = keep
    leaving = summed.reshape(count_x, kx, count_y, ky, count_z, kz, 2, share, cheb)
    leaving = leaving.transpose(0, 2, 4, 1, 3, 5, 6, 7, 8)
    leaving = leaving.reshape(count_x, count_yz, kx, ky, kz, 2, 1, share, cheb)
    back = lax.all_to_all(leaving, "gx", split_axis=0, concat_axis=6, tiled=True)
    back = lax.all_to_all(back, ("gy", "gz"), split_axis=1, concat_axis=7, tiled=True)
    back = back.reshape(kx, ky, kz, 2, lx, ly, lz, rhs, cheb)

    mats = translation.reshape(2, 2, 2, cheb, cheb)
    for d, (c, name) in enumerate(zip(counts, AXES)):
        if c > q:
            mats = lax.dynamic_index_in_dim(mats, lax.axis_index(name) % 2, d, keepdims=True)
    return last_translate(back, mats, weights.shape)


def last_kernel(e_ref, t_ref, o_ref):
    rows = e_ref[0, 0]
    lx, ly, kz, nz, m, cheb = (o_ref.shape[1],) + tuple(o_ref.shape[3:])
    for z in range(nz):
        r = jnp.dot(rows, t_ref[0, 0, z], preferred_element_type=jnp.float32)
        o_ref[0, :, 0, :, :, z] = r.astype(jnp.bfloat16).reshape(lx, ly, kz, m, cheb)


def last_translate(back, mats, out_shape):
    kx, ky, kz, _, lx, ly, lz, rhs, cheb = back.shape
    nx, ny, nz = mats.shape[:3]
    m = lz * 2 * rhs
    rows = back.transpose(0, 1, 4, 5, 2, 6, 3, 7, 8).reshape(kx, ky, lx * ly * kz * m, cheb)
    out = pl.pallas_call(
        last_kernel,
        grid=(nx, ny, kx, ky),
        in_specs=[
            pl.BlockSpec((1, 1, lx * ly * kz * m, cheb), lambda x, y, a, b: (a, b, 0, 0)),
            pl.BlockSpec((1, 1, nz, cheb, cheb), lambda x, y, a, b: (x, y, 0, 0, 0)),
        ],
        out_specs=pl.BlockSpec(
            (1, lx, 1, ly, kz, nz, m, cheb),
            lambda x, y, a, b: (a * nx + x, 0, b * ny + y, 0, 0, 0, 0, 0),
        ),
        out_shape=jax.ShapeDtypeStruct(
            (kx * nx, lx, ky * ny, ly, kz, nz, m, cheb), jnp.bfloat16
        ),
        compiler_params=pltpu.CompilerParams(vmem_limit_bytes=40 * 2**20),
        name="last_translate",
    )(rows, mats)
    return out.reshape(out_shape)


def first_kernel(w_ref, a_ref, re_ref, im_ref, cos_ref, sin_ref):
    ly, count_z = a_ref.shape[3], a_ref.shape[4]
    lz = re_ref.shape[5]
    cosine, sine = sincos(a_ref[0, 0, 0])
    cos_ref[...] = cosine
    sin_ref[...] = sine

    @pl.loop(0, ly)
    def _(l):
        for z in range(count_z):
            c = cos_ref[l, z : z + 1, :]
            s = sin_ref[l, z : z + 1, :]
            re = w_ref[0, 0, 0, l, z, 0].astype(jnp.float32)
            im = w_ref[0, 0, 0, l, z, 1].astype(jnp.float32)
            re_ref[0, 0, z // lz, 0, l, z % lz] = (re * c - im * s).astype(jnp.bfloat16)
            im_ref[0, 0, z // lz, 0, l, z % lz] = (re * s + im * c).astype(jnp.bfloat16)


def first_rotate(weights, angle, low):
    lx, ly, lz = low
    sx, sy, sz, _, rhs, cheb = weights.shape
    hx, hy, hz = sx // lx, sy // ly, sz // lz
    shape = (hx, hy, hz, lx, ly, lz, rhs, cheb)
    out = jax.ShapeDtypeStruct(shape, jnp.bfloat16)
    spec = pl.BlockSpec(
        (1, 1, hz, 1, ly, lz, rhs, cheb), lambda a, x, b: (a, b, 0, x, 0, 0, 0, 0)
    )
    return pl.pallas_call(
        first_kernel,
        grid=(hx, lx, hy),
        in_specs=[
            pl.BlockSpec(
                (1, 1, 1, ly, sz, 2, rhs, cheb), lambda a, x, b: (a, x, b, 0, 0, 0, 0, 0)
            ),
            pl.BlockSpec((1, 1, 1, ly, sz, cheb), lambda a, x, b: (a, x, b, 0, 0, 0)),
        ],
        out_specs=[spec, spec],
        out_shape=[out, out],
        scratch_shapes=[pltpu.VMEM((ly, sz, cheb), jnp.float32)] * 2,
        compiler_params=pltpu.CompilerParams(vmem_limit_bytes=40 * 2**20),
        name="first_rotate",
    )(
        weights.reshape(hx, lx, hy, ly, sz, 2, rhs, cheb),
        angle.reshape(hx, lx, hy, ly, sz, cheb),
    )


def solution(mesh):
    in_specs = (P("gx", "gy", "gz", None, None, None), P(None, "gx", "gy", "gz", None), P())
    out_specs = P("gx", "gy", "gz", None, None, None)
    return jax.shard_map(shards, mesh=mesh, in_specs=in_specs, out_specs=out_specs, check_vma=False)
```

time: 1650 us -> 553 us (0.34)
  blocking collectives: 554 us -> 89.2 us
  waiting for transfers between devices: 638 us -> 216 us
  local copies, waits for them, and re-layouts: 237 us -> 84.2 us
  other arithmetic: 151 us -> 54.2 us
  Pallas kernels: 0 us -> 36 us
  matrix products: 42.2 us -> 25.5 us
    all_to_all x4 -> x3, waiting for transfers between devices: 638 us -> 21.2 us  [the longest x1 21.2 us: exchange_low(): lax.all_to_all(terms, axis_name, split_axis=dim, concat_axis=dim, axis_in...]
    all_to_all x2 -> x3, blocking collectives: 554 us -> 89.2 us  [the longest x1 53.3 us: shards(): lax.all_to_all(leaving, 'gx', split_axis=0, concat_axis=6, tiled=True)]
    ppermute x0 -> x18, waiting for transfers between devices: none -> 195 us  [halve_sum(): got = lax.ppermute(theirs, axis_name, pairs)]
    another operation x24 -> x2, other arithmetic: 110 us -> 0.23 us  [shards(): jnp.stack([jnp.concatenate([streams[p, k] for k in range(3) if (p, k) in...]
    another operation x8 -> x1, local copies, waits for them, and re-layouts: 58.6 us -> 1.85 us  [shards(): ph.reshape(1, 1, hx, hy, hz, LEVELS - 1, count_x, blocks * repeat // coun...]
    all_to_all x6 -> x5, local copies, waits for them, and re-layouts: 60.7 us -> 7.46 us  [the longest x1 2.97 us: shards(): ph = lax.all_to_all(ph, 'gx', split_axis=6, concat_axis=0, tiled=True)]
    cos x4 -> x0, local copies, waits for them, and re-layouts: 51.3 us -> none  [rotate_blocks(): cosine = jnp.cos(angle)[:, :, :, :, None, :]]
    pallas_call x0 -> x2, Pallas kernels: none -> 36 us  [the longest x1 24.4 us: first_rotate(): pl.pallas_call(first_kernel, grid=(hx, lx, hy), in_specs=[pl.BlockSpec((1...]
  transfers between devices with their start and end apart: 4 -> 21, of which waited for: 4 -> 10; matrix products, arithmetic and copies ran while one was open for 7% -> 14% of each run, Pallas kernels for 0% -> 0%
where the time goes in v1:
time: 553 us; the launch traced here: 545 us
  waiting for transfers between devices  216 us (39%)
  blocking collectives  89.2 us (16%)
  local copies, waits for them, and re-layouts  84.2 us (15%)
  other arithmetic  54.2 us (10%)
  starting transfers between devices  38.4 us (7%)
  Pallas kernels  36 us (7%)
  matrix products  25.5 us (5%)
    ppermute x18, waiting for transfers between devices, halve_sum(): got = lax.ppermute(theirs, axis_name, pairs)  195 us
    all_to_all x1, blocking collectives, shards(): lax.all_to_all(leaving, 'gx', split_axis=0, concat_axis=6, tiled=True)  53.3 us
    all_to_all x1, blocking collectives, shards(): lax.all_to_all(back, ('gy', 'gz'), split_axis=1, concat_axis=7, tiled=True)  29.6 us
    dot_general x2, matrix products, translate(): jnp.einsum('crk,tkn->ctrn', s, translation, preferred_element_type=jnp.fl...  25.5 us
    pallas_call x1, Pallas kernels, first_rotate(): pl.pallas_call(first_kernel, grid=(hx, lx, hy), in_specs=[pl.BlockSpec((1...  24.4 us
    ppermute x18, starting transfers between devices, halve_sum(): got = lax.ppermute(theirs, axis_name, pairs)  24.3 us
    all_to_all x1, waiting for transfers between devices, exchange_low(): lax.all_to_all(terms, axis_name, split_axis=dim, concat_axis=dim, axis_in...  21.2 us
    slice x2, local copies, waits for them, and re-layouts, rotate_sum(): im = current[1].astype(jnp.float32)  18 us
  transfers between devices with their start and end apart: 21, of which 10 were waited for; matrix products, arithmetic and copies ran while one was open for 14% of the time, Pallas kernels for 0%

profile of v1, /device:TPU:0, one launch (start us, length us, event | category | flops | bytes accessed | tf_op | source)
XLA Modules:
  0.0 545.2 jit_solution(8783615864773938586)
XLA Ops:
  1.8 24.4 %first_rotate.1 = (bf16[2,4,2,4,4,4,8,512]{7,6,5,4,3,2,1,0:T(8,128)(2,1)S(1)}, bf16[2,4,2,4,4,4,8,512]{7,6,5,4,3,2,1,0:T(8,128)(2,1)}) custom-call(bf16[2,4,4,4,8,2,8,512]{7,6,5,4,3,2,1,0:T(8,128)(2,1)} %bitcast.126, f32[2,4,4,4,8,512]{5,4,3,2,1,0:T(8,128)S(1)} %bitcast.109), custom_call_target="tpu_custom_call" | custom-call | tf_op jit(solution)/shard_map/first_rotate/pallas_call | solution.py:213
  26.2 2.3 fusion.20
  28.5 3.2 copy-done
  33.5 3.4 fusion.21
  36.9 4.8 constant_dynamic-slice_fusion.11
  42.9 4.1 collective-permute-start
  46.9 3.9 constant_dynamic-slice_fusion.7
  55.0 2.2 slice.65
  57.2 4.1 slice.68
  61.4 4.3 constant_dynamic-slice_fusion.3
  69.3 3.8 slice.79
  73.1 2.5 reshape.119
  75.7 2.8 copy.70
  80.3 5.3 all-to-all-start.2
  87.3 68.2 %collective-permute-done = bf16[5,1,2,2,1,2,2,16,512]{8,7,6,0,2,5,4,3,1:T(8,128)(2,1)} collective-permute-done((bf16[5,1,2,2,1,2,2,16,512]{8,7,6,0,2,5,4,3,1:T(8,128)(2,1)}, bf16[5,1,2,2,1,2,2,16,512]{8,7,6,0,2,5,4,3,1:T(8,128)(2,1)}, u32[]{:S(2)}, u32[]{:S(2)}) %collective-permute-start) | collective-permute-done | bytes 1310752 | tf_op jit(solution)/shard_map/ppermute | solution.py:31
  157.4 2.0 add_convert_fusion.5
  161.0 2.0 add_convert_fusion.4
  163.0 20.6 %collective-permute-done.9 = bf16[5,1,2,2,1,2,2,16,512]{8,7,6,0,2,5,4,3,1:T(8,128)(2,1)} collective-permute-done((bf16[5,1,2,2,1,2,2,16,512]{8,7,6,0,2,5,4,3,1:T(8,128)(2,1)}, bf16[5,1,2,2,1,2,2,16,512]{8,7,6,0,2,5,4,3,1:T(8,128)(2,1)}, u32[]{:S(2)}, u32[]{:S(2)}) %collective-permute-start.9) | collective-permute-done | bytes 1310752 | tf_op jit(solution)/shard_map/ppermute | solution.py:31
  185.5 2.0 add_convert_fusion.3
  189.1 2.0 add_convert_fusion.2
  191.7 2.2 add_convert_fusion.1
  195.0 3.0 collective-permute-start.16
  198.2 8.6 %collective-permute-done.4 = bf16[5,2,2,1,1,1,2,16,512]{8,7,6,0,2,5,4,3,1:T(8,128)(2,1)S(1)} collective-permute-done((bf16[5,2,2,1,1,1,2,16,512]{8,7,6,0,2,5,4,3,1:T(8,128)(2,1)S(1)}, bf16[5,2,2,1,1,1,2,16,512]{8,7,6,0,2,5,4,3,1:T(8,128)(2,1)S(1)}, u32[]{:S(2)}, u32[]{:S(2)}) %collective-permute-start.4) | collective-permute-done | bytes 655392 | tf_op jit(solution)/shard_map/ppermute | solution.py:31
  209.4 11.5 %collective-permute-done.13 = bf16[5,2,2,1,1,1,2,16,512]{8,7,6,0,2,5,4,3,1:T(8,128)(2,1)S(1)} collective-permute-done((bf16[5,2,2,1,1,1,2,16,512]{8,7,6,0,2,5,4,3,1:T(8,128)(2,1)S(1)}, bf16[5,2,2,1,1,1,2,16,512]{8,7,6,0,2,5,4,3,1:T(8,128)(2,1)S(1)}, u32[]{:S(2)}, u32[]{:S(2)}) %collective-permute-start.13) | collective-permute-done | bytes 655392 | tf_op jit(solution)/shard_map/ppermute | solution.py:31
  223.0 4.9 collective-permute-done.2
  228.0 66.4 %collective-permute-done.5 = bf16[5,1,2,1,1,1,2,16,512]{8,7,6,0,2,5,4,3,1:T(8,128)(2,1)S(1)} collective-permute-done((bf16[5,1,2,1,1,1,2,16,512]{8,7,6,0,2,5,4,3,1:T(8,128)(2,1)S(1)}, bf16[5,1,2,1,1,1,2,16,512]{8,7,6,0,2,5,4,3,1:T(8,128)(2,1)S(1)}, u32[]{:S(2)}, u32[]{:S(2)}) %collective-permute-start.5) | collective-permute-done | bytes 327712 | tf_op jit(solution)/shard_map/ppermute | solution.py:31
  297.6 3.0 collective-permute-done.14
  300.7 6.4 %collective-permute-done.8 = bf16[6,1,2,1,1,1,2,16,512]{8,7,6,0,2,5,4,3,1:T(8,128)(2,1)S(1)} collective-permute-done((bf16[6,1,2,1,1,1,2,16,512]{8,7,6,0,2,5,4,3,1:T(8,128)(2,1)S(1)}, bf16[6,1,2,1,1,1,2,16,512]{8,7,6,0,2,5,4,3,1:T(8,128)(2,1)S(1)}, u32[]{:S(2)}, u32[]{:S(2)}) %collective-permute-start.8) | collective-permute-done | bytes 393248 | tf_op jit(solution)/shard_map/ppermute | solution.py:31
  307.4 5.6 %collective-permute-done.17 = bf16[6,1,2,1,1,1,2,16,512]{8,7,6,0,2,5,4,3,1:T(8,128)(2,1)S(1)} collective-permute-done((bf16[6,1,2,1,1,1,2,16,512]{8,7,6,0,2,5,4,3,1:T(8,128)(2,1)S(1)}, bf16[6,1,2,1,1,1,2,16,512]{8,7,6,0,2,5,4,3,1:T(8,128)(2,1)S(1)}, u32[]{:S(2)}, u32[]{:S(2)}) %collective-permute-start.17) | collective-permute-done | bytes 393248 | tf_op jit(solution)/shard_map/ppermute | solution.py:31
  314.8 4.8 all-to-all-start
  319.6 3.0 copy.72
  322.6 21.2 %all-to-all-done = bf16[2,16,2,1,2,16,512]{6,5,4,1,0,3,2:T(8,128)(2,1)} async-done(((bf16[2,16,2,1,2,16,512]{6,5,4,1,0,3,2:T(8,128)(2,1)}), bf16[2,16,2,1,2,16,512]{6,5,4,1,0,3,2:T(8,128)(2,1)}, u32[]{:S(2)}, u32[]{:S(2)}) %all-to-all-start) | async-done | bytes 2097184 | tf_op jit(solution)/shard_map/all_to_all | solution.py:41
  345.6 6.3 %all_to_all.76 = bf16[2,16,2,1,2,16,512]{6,5,2,1,0,3,4:T(8,128)(2,1)} all-to-all(bf16[2,16,2,1,2,16,512]{6,5,2,1,0,3,4:T(8,128)(2,1)S(1)} %copy.68), channel_id=1, replica_groups={{0,1},{2,3},{4,5},{6,7},{8,9},{10,11},{12,13},{14,15},{16,17},{18,19},{..., dimensions={4} | all-to-all | bytes 4194304 | tf_op jit(solution)/shard_map/all_to_all | solution.py:41
  351.9 3.9 all-to-all-start.3
  358.7 11.8 %convert_bitcast_fusion.1 = bf16[2,8,1024,512]{3,2,1,0:T(8,128)(2,1)} fusion(bf16[2,1024,512,1]{2,1,3,0:T(8,128)(2,1)S(1)} %bitcast.141, bf16[8,512,512]{2,1,0:T(8,128)(2,1)S(1)} %copy-done.1), kind=kOutput, calls=%fused_computation.17 | convolution fusion | flops 8598323200 | bytes 23068672 | tf_op jit(solution)/shard_map/crk,tkn->ctrn/dot_general | solution.py:114
  370.5 11.4 %fusion.19 = (bf16[1,8,1024,512]{3,2,1,0:T(8,128)(2,1)}, bf16[1,8,1024,512]{3,2,1,0:T(8,128)(2,1)}) fusion(bf16[2,8,1024,512]{3,2,1,0:T(8,128)(2,1)} %convert_bitcast_fusion.1), kind=kLoop, calls=%fused_computation.90 | loop fusion | bytes 33554432 | tf_op jit(solution)/shard_map/slice | solution.py:51
  381.8 2.2 copy.73
  384.0 2.7 copy.128
  386.8 2.5 convert_multiply_fusion.8
  390.4 5.4 fusion.10
  395.9 13.4 %fusion.1 = (bf16[2,2,2,2,2,2,2,8,512]{8,7,6,5,4,3,2,1,0:T(8,128)(2,1)S(1)}, bf16[2,2,2,2,2,2,2,8,512]{8,7,6,5,4,3,2,1,0:T(8,128)(2,1)}) fusion(bf16[2,2,2,2,2,2,2,2,2,2,8,512]{11,10,9,8,7,6,5,4,3,2,1,0:T(8,128)(2,1)S(1)} %bitcast.119, bf16[2,2,2,2,2,2,2,2,2,2,8,512]{11,10,9,8,7,6,5,4,3,2,1,0:T(8,128)(2,1)S(1)} %bitcast.116, ...), kind=kLoop, calls=%fused_computation.9 | loop fusion | flops 48758784 | bytes 25165824 | tf_op jit(solution)/shard_map/reduce_sum | solution.py:124
  409.3 13.7 %convert_bitcast_fusion = bf16[2,8,1024,512]{3,2,1,0:T(8,128)(2,1)} fusion(bf16[8,512,512]{2,1,0:T(8,128)(2,1)S(1)} %copy-done.2, bf16[1,1024,512]{2,1,0:T(8,128)(2,1)} %bitcast.143, bf16[1,1024,512]{2,1,0:T(8,128)(2,1)S(1)} %bitcast.142), kind=kOutput, calls=%fused_computation.16 | convolution fusion | flops 8602517504 | bytes 23068672 | tf_op jit(solution)/shard_map/crk,tkn->ctrn/dot_general | solution.py:114
  423.0 6.6 %fusion.18 = (bf16[1,8,1024,512]{3,2,1,0:T(8,128)(2,1)S(1)}, bf16[1,8,1024,512]{3,2,1,0:T(8,128)(2,1)S(1)}) fusion(bf16[2,8,1024,512]{3,2,1,0:T(8,128)(2,1)} %convert_bitcast_fusion), kind=kLoop, calls=%fused_computation.89 | loop fusion | bytes 33554432 | tf_op jit(solution)/shard_map/slice | solution.py:51
  430.8 5.4 fusion.11
  436.3 12.4 %fusion.5 = (bf16[2,2,2,2,2,2,2,8,512]{8,7,6,5,4,3,2,1,0:T(8,128)(2,1)S(1)}, bf16[2,2,2,2,2,2,2,8,512]{8,7,6,5,4,3,2,1,0:T(8,128)(2,1)S(1)}) fusion(bf16[2,2,2,2,2,2,2,2,2,2,8,512]{11,10,9,8,7,6,5,4,3,2,1,0:T(8,128)(2,1)S(1)} %bitcast.121, bf16[2,2,2,2,2,2,2,2,2,2,8,512]{11,10,9,8,7,6,5,4,3,2,1,0:T(8,128)(2,1)S(1)} %bitcast.120, ...), kind=kLoop, calls=%fused_computation.13 | loop fusion | flops 48758784 | bytes 25165824 | tf_op jit(solution)/shard_map/reduce_sum | solution.py:130
  449.4 53.3 %all_to_all.77 = bf16[4,8,1,2,1,2,1,16,512]{8,7,5,3,1,6,4,2,0:T(8,128)(2,1)S(1)} all-to-all(bf16[4,8,1,2,1,2,1,16,512]{8,7,5,3,1,6,4,2,0:T(8,128)(2,1)S(1)} %bitcast.136), channel_id=1, replica_groups=mesh['gx'=4,'gy'=2,'gz'=4] {'gx'}, dimensions={0} | all-to-all | bytes 4194304 | tf_op jit(solution)/shard_map/all_to_all | solution.py:142
  503.1 29.6 %all_to_all.78 = bf16[1,8,1,2,1,2,4,16,512]{8,7,5,3,6,4,2,0,1:T(8,128)(2,1)S(1)} all-to-all(bf16[1,8,1,2,1,2,4,16,512]{8,7,5,3,6,4,2,0,1:T(8,128)(2,1)S(1)} %copy.85), channel_id=1, replica_groups=mesh['gx'=4,'gy'=2,'gz'=4] {'gy','gz'}, dimensions={1} | all-to-all | bytes 4194304 | tf_op jit(solution)/shard_map/all_to_all | solution.py:143
  533.2 11.6 %last_translate.1 = bf16[2,4,4,4,1,2,64,512]{7,6,5,4,3,2,1,0:T(8,128)(2,1)} custom-call(bf16[1,2,1024,512]{3,2,1,0:T(8,128)(2,1)S(1)} %bitcast.112, bf16[2,2,2,512,512]{4,3,2,1,0:T(8,128)(2,1)S(1)} %bitcast.113), custom_call_target="tpu_custom_call" | custom-call | tf_op jit(solution)/shard_map/last_translate/pallas_call | solution.py:166
  (108 shorter events, 43.4 us)
Async XLA Ops:
  26.2 5.5 %copy-start = (bf16[2,4,2,4,4,4,8,512]{7,6,5,4,3,2,1,0:T(8,128)(2,1)}, bf16[2,4,2,4,4,4,8,512]{7,6,5,4,3,2,1,0:T(8,128)(2,1)S(1)}, u32[]{:S(2)}) copy-start(bf16[2,4,2,4,4,4,8,512]{7,6,5,4,3,2,1,0:T(8,128)(2,1)S(1)} %get-tuple-element.7) | copy-start | bytes 25165828
  26.2 7.3 %copy-start.4 = (bf16[2,4,2,4,4,4,8,512]{7,6,5,4,3,2,1,0:T(8,128)(2,1)S(1)}, bf16[2,4,2,4,4,4,8,512]{7,6,5,4,3,2,1,0:T(8,128)(2,1)}, u32[]{:S(2)}) copy-start(bf16[2,4,2,4,4,4,8,512]{7,6,5,4,3,2,1,0:T(8,128)(2,1)} %get-tuple-element.8) | copy-start | bytes 25165828
  42.9 112.7 %collective-permute-start = (bf16[5,1,2,2,1,2,2,16,512]{8,7,6,0,2,5,4,3,1:T(8,128)(2,1)}, bf16[5,1,2,2,1,2,2,16,512]{8,7,6,0,2,5,4,3,1:T(8,128)(2,1)}, u32[]{:S(2)}, u32[]{:S(2)}) collective-permute-start(bf16[5,1,2,2,1,2,2,16,512]{8,7,6,0,2,5,4,3,1:T(8,128)(2,1)} %copy.92), channel_id=1, source_target_pairs={{0,16},{8,24},{16,0},{24,8},{1,17},{9,25},{17,1},{25,9},{2,18},{10... | collective-permute-start | bytes 3932168 | tf_op jit(solution)/shard_map/ppermute | solution.py:31
  50.8 2.7 copy-start.8
  52.0 107.4 %collective-permute-start.3 = (bf16[5,2,2,1,1,2,2,16,512]{8,7,6,0,2,5,4,3,1:T(8,128)(2,1)}, bf16[5,2,2,1,1,2,2,16,512]{8,7,6,0,2,5,4,3,1:T(8,128)(2,1)}, u32[]{:S(2)}, u32[]{:S(2)}) collective-permute-start(bf16[5,2,2,1,1,2,2,16,512]{8,7,6,0,2,5,4,3,1:T(8,128)(2,1)} %copy.95), channel_id=1, source_target_pairs={{0,4},{4,0},{1,5},{5,1},{2,6},{6,2},{3,7},{7,3},{8,12},{12,8},{9,1... | collective-permute-start | bytes 3932168 | tf_op jit(solution)/shard_map/ppermute | solution.py:31
  54.7 128.9 %collective-permute-start.9 = (bf16[5,1,2,2,1,2,2,16,512]{8,7,6,0,2,5,4,3,1:T(8,128)(2,1)}, bf16[5,1,2,2,1,2,2,16,512]{8,7,6,0,2,5,4,3,1:T(8,128)(2,1)}, u32[]{:S(2)}, u32[]{:S(2)}) collective-permute-start(bf16[5,1,2,2,1,2,2,16,512]{8,7,6,0,2,5,4,3,1:T(8,128)(2,1)} %copy.101), channel_id=1, source_target_pairs={{0,16},{8,24},{16,0},{24,8},{1,17},{9,25},{17,1},{25,9},{2,18},{10... | collective-permute-start | bytes 3932168 | tf_op jit(solution)/shard_map/ppermute | solution.py:31
  65.7 2.9 copy-start.7
  67.0 124.1 %collective-permute-start.6 = (bf16[6,2,2,2,1,1,2,16,512]{8,7,6,0,2,5,4,3,1:T(8,128)(2,1)}, bf16[6,2,2,2,1,1,2,16,512]{8,7,6,0,2,5,4,3,1:T(8,128)(2,1)}, u32[]{:S(2)}, u32[]{:S(2)}) collective-permute-start(bf16[6,2,2,2,1,1,2,16,512]{8,7,6,0,2,5,4,3,1:T(8,128)(2,1)} %copy.98), channel_id=1, source_target_pairs={{0,2},{1,3},{2,0},{3,1},{4,6},{5,7},{6,4},{7,5},{8,10},{9,11},{10,... | collective-permute-start | bytes 4718600 | tf_op jit(solution)/shard_map/ppermute | solution.py:31
  68.6 118.8 %collective-permute-start.12 = (bf16[5,2,2,1,1,2,2,16,512]{8,7,6,0,2,5,4,3,1:T(8,128)(2,1)S(1)}, bf16[5,2,2,1,1,2,2,16,512]{8,7,6,0,2,5,4,3,1:T(8,128)(2,1)}, u32[]{:S(2)}, u32[]{:S(2)}) collective-permute-start(bf16[5,2,2,1,1,2,2,16,512]{8,7,6,0,2,5,4,3,1:T(8,128)(2,1)S(1)} %copy.104), channel_id=1, source_target_pairs={{0,4},{4,0},{1,5},{5,1},{2,6},{6,2},{3,7},{7,3},{8,12},{12,8},{9,1... | collective-permute-start | bytes 3932168 | tf_op jit(solution)/shard_map/ppermute | solution.py:31
  80.3 234.5 %all-to-all-start.2 = ((bf16[1,1,2,4,2,2,4,16,512]{8,7,5,4,3,2,1,0,6:T(8,128)(2,1)}), bf16[1,1,2,4,2,2,4,16,512]{8,7,5,4,3,2,1,0,6:T(8,128)(2,1)S(1)}, u32[]{:S(2)}, u32[]{:S(2)}) async-start(bf16[1,1,2,4,2,2,4,16,512]{8,7,5,4,3,2,1,0,6:T(8,128)(2,1)} %copy.71), calls=%async_computation.2 | async-start | bytes 4194304 | tf_op jit(solution)/shard_map/all_to_all | solution.py:78
  85.6 71.7 %copy-start.11 = (bf16[5,1,2,2,1,2,2,16,512]{8,7,6,5,3,2,1,0,4:T(8,128)(2,1)S(1)}, bf16[5,1,2,2,1,2,2,16,512]{8,7,6,5,3,2,1,0,4:T(8,128)(2,1)}, u32[]{:S(2)}) copy-start(bf16[5,1,2,2,1,2,2,16,512]{8,7,6,5,3,2,1,0,4:T(8,128)(2,1)} %get-tuple-element.42) | copy-start | bytes 3932164
  155.5 38.5 %collective-permute-start.15 = (bf16[6,2,2,2,1,1,2,16,512]{8,7,6,0,2,5,4,3,1:T(8,128)(2,1)S(1)}, bf16[6,2,2,2,1,1,2,16,512]{8,7,6,0,2,5,4,3,1:T(8,128)(2,1)S(1)}, u32[]{:S(2)}, u32[]{:S(2)}) collective-permute-start(bf16[6,2,2,2,1,1,2,16,512]{8,7,6,0,2,5,4,3,1:T(8,128)(2,1)S(1)} %copy.107), channel_id=1, source_target_pairs={{0,2},{1,3},{2,0},{3,1},{4,6},{5,7},{6,4},{7,5},{8,10},{9,11},{10,... | collective-permute-start | bytes 4718600 | tf_op jit(solution)/shard_map/ppermute | solution.py:31
  157.4 3.6 copy-start.12
  159.4 35.5 %collective-permute-start.1 = (bf16[5,1,2,1,1,2,2,16,512]{8,7,6,0,2,5,4,3,1:T(8,128)(2,1)S(1)}, bf16[5,1,2,1,1,2,2,16,512]{8,7,6,0,2,5,4,3,1:T(8,128)(2,1)S(1)}, u32[]{:S(2)}, u32[]{:S(2)}) collective-permute-start(bf16[5,1,2,1,1,2,2,16,512]{8,7,6,0,2,5,4,3,1:T(8,128)(2,1)S(1)} %constant_dynamic-slice_fusion.21), channel_id=1, source_target_pairs={{0,4},{4,0},{1,5},{5,1},{2,6},{6,2},{3,7},{7,3},{8,12},{12,8},{9,1... | collective-permute-start | bytes 1966088 | tf_op jit(solution)/shard_map/ppermute | solution.py:31
  161.0 24.5 %copy-start.9 = (bf16[5,1,2,2,1,2,2,16,512]{8,7,6,5,3,2,1,0,4:T(8,128)(2,1)S(1)}, bf16[5,1,2,2,1,2,2,16,512]{8,7,6,5,3,2,1,0,4:T(8,128)(2,1)}, u32[]{:S(2)}) copy-start(bf16[5,1,2,2,1,2,2,16,512]{8,7,6,5,3,2,1,0,4:T(8,128)(2,1)} %get-tuple-element.33) | copy-start | bytes 3932164
  183.6 23.2 %collective-permute-start.4 = (bf16[5,2,2,1,1,1,2,16,512]{8,7,6,0,2,5,4,3,1:T(8,128)(2,1)S(1)}, bf16[5,2,2,1,1,1,2,16,512]{8,7,6,0,2,5,4,3,1:T(8,128)(2,1)S(1)}, u32[]{:S(2)}, u32[]{:S(2)}) collective-permute-start(bf16[5,2,2,1,1,1,2,16,512]{8,7,6,0,2,5,4,3,1:T(8,128)(2,1)S(1)} %constant_dynamic-slice_fusion.17), channel_id=1, source_target_pairs={{0,2},{1,3},{2,0},{3,1},{4,6},{5,7},{6,4},{7,5},{8,10},{9,11},{10,... | collective-permute-start | bytes 1966088 | tf_op jit(solution)/shard_map/ppermute | solution.py:31
  185.4 3.6 copy-start.10
  187.5 21.5 %collective-permute-start.10 = (bf16[5,1,2,1,1,2,2,16,512]{8,7,6,0,2,5,4,3,1:T(8,128)(2,1)S(1)}, bf16[5,1,2,1,1,2,2,16,512]{8,7,6,0,2,5,4,3,1:T(8,128)(2,1)S(1)}, u32[]{:S(2)}, u32[]{:S(2)}) collective-permute-start(bf16[5,1,2,1,1,2,2,16,512]{8,7,6,0,2,5,4,3,1:T(8,128)(2,1)S(1)} %constant_dynamic-slice_fusion.9), channel_id=1, source_target_pairs={{0,4},{4,0},{1,5},{5,1},{2,6},{6,2},{3,7},{7,3},{8,12},{12,8},{9,1... | collective-permute-start | bytes 1966088 | tf_op jit(solution)/shard_map/ppermute | solution.py:31
  189.1 2.6 copy-start.6
  191.1 29.8 %collective-permute-start.13 = (bf16[5,2,2,1,1,1,2,16,512]{8,7,6,0,2,5,4,3,1:T(8,128)(2,1)S(1)}, bf16[5,2,2,1,1,1,2,16,512]{8,7,6,0,2,5,4,3,1:T(8,128)(2,1)S(1)}, u32[]{:S(2)}, u32[]{:S(2)}) collective-permute-start(bf16[5,2,2,1,1,1,2,16,512]{8,7,6,0,2,5,4,3,1:T(8,128)(2,1)S(1)} %constant_dynamic-slice_fusion.5), channel_id=1, source_target_pairs={{0,2},{1,3},{2,0},{3,1},{4,6},{5,7},{6,4},{7,5},{8,10},{9,11},{10,... | collective-permute-start | bytes 1966088 | tf_op jit(solution)/shard_map/ppermute | solution.py:31
  191.7 2.4 copy-start.5
  194.0 100.7 %collective-permute-start.7 = (bf16[6,1,2,2,1,1,2,16,512]{8,7,6,0,2,5,4,3,1:T(8,128)(2,1)S(1)}, bf16[6,1,2,2,1,1,2,16,512]{8,7,6,0,2,5,4,3,1:T(8,128)(2,1)S(1)}, u32[]{:S(2)}, u32[]{:S(2)}) collective-permute-start(bf16[6,1,2,2,1,1,2,16,512]{8,7,6,0,2,5,4,3,1:T(8,128)(2,1)S(1)} %constant_dynamic-slice_fusion.13), channel_id=1, source_target_pairs={{0,16},{8,24},{16,0},{24,8},{1,17},{9,25},{17,1},{25,9},{2,18},{10... | collective-permute-start | bytes 2359304 | tf_op jit(solution)/shard_map/ppermute | solution.py:31
  195.0 102.0 %collective-permute-start.16 = (bf16[6,1,2,2,1,1,2,16,512]{8,7,6,0,2,5,4,3,1:T(8,128)(2,1)S(1)}, bf16[6,1,2,2,1,1,2,16,512]{8,7,6,0,2,5,4,3,1:T(8,128)(2,1)S(1)}, u32[]{:S(2)}, u32[]{:S(2)}) collective-permute-start(bf16[6,1,2,2,1,1,2,16,512]{8,7,6,0,2,5,4,3,1:T(8,128)(2,1)S(1)} %constant_dynamic-slice_fusion.1), channel_id=1, source_target_pairs={{0,16},{8,24},{16,0},{24,8},{1,17},{9,25},{17,1},{25,9},{2,18},{10... | collective-permute-start | bytes 2359304 | tf_op jit(solution)/shard_map/ppermute | solution.py:31
  206.8 21.1 %collective-permute-start.2 = (bf16[5,1,2,1,1,1,2,16,512]{8,7,6,0,2,5,4,3,1:T(8,128)(2,1)S(1)}, bf16[5,1,2,1,1,1,2,16,512]{8,7,6,0,2,5,4,3,1:T(8,128)(2,1)S(1)}, u32[]{:S(2)}, u32[]{:S(2)}) collective-permute-start(bf16[5,1,2,1,1,1,2,16,512]{8,7,6,0,2,5,4,3,1:T(8,128)(2,1)S(1)} %constant_dynamic-slice_fusion.20), channel_id=1, source_target_pairs={{0,2},{1,3},{2,0},{3,1},{4,6},{5,7},{6,4},{7,5},{8,10},{9,11},{10,... | collective-permute-start | bytes 983048 | tf_op jit(solution)/shard_map/ppermute | solution.py:31
  209.0 85.5 %collective-permute-start.5 = (bf16[5,1,2,1,1,1,2,16,512]{8,7,6,0,2,5,4,3,1:T(8,128)(2,1)S(1)}, bf16[5,1,2,1,1,1,2,16,512]{8,7,6,0,2,5,4,3,1:T(8,128)(2,1)S(1)}, u32[]{:S(2)}, u32[]{:S(2)}) collective-permute-start(bf16[5,1,2,1,1,1,2,16,512]{8,7,6,0,2,5,4,3,1:T(8,128)(2,1)S(1)} %constant_dynamic-slice_fusion.16), channel_id=1, source_target_pairs={{0,16},{8,24},{16,0},{24,8},{1,17},{9,25},{17,1},{25,9},{2,18},{10... | collective-permute-start | bytes 983048 | tf_op jit(solution)/shard_map/ppermute | solution.py:31
  220.9 73.7 %collective-permute-start.11 = (bf16[5,1,2,1,1,1,2,16,512]{8,7,6,0,2,5,4,3,1:T(8,128)(2,1)S(1)}, bf16[5,1,2,1,1,1,2,16,512]{8,7,6,0,2,5,4,3,1:T(8,128)(2,1)S(1)}, u32[]{:S(2)}, u32[]{:S(2)}) collective-permute-start(bf16[5,1,2,1,1,1,2,16,512]{8,7,6,0,2,5,4,3,1:T(8,128)(2,1)S(1)} %constant_dynamic-slice_fusion.8), channel_id=1, source_target_pairs={{0,2},{1,3},{2,0},{3,1},{4,6},{5,7},{6,4},{7,5},{8,10},{9,11},{10,... | collective-permute-start | bytes 983048 | tf_op jit(solution)/shard_map/ppermute | solution.py:31
  227.9 72.7 %collective-permute-start.14 = (bf16[5,1,2,1,1,1,2,16,512]{8,7,6,0,2,5,4,3,1:T(8,128)(2,1)S(1)}, bf16[5,1,2,1,1,1,2,16,512]{8,7,6,0,2,5,4,3,1:T(8,128)(2,1)S(1)}, u32[]{:S(2)}, u32[]{:S(2)}) collective-permute-start(bf16[5,1,2,1,1,1,2,16,512]{8,7,6,0,2,5,4,3,1:T(8,128)(2,1)S(1)} %constant_dynamic-slice_fusion.4), channel_id=1, source_target_pairs={{0,16},{8,24},{16,0},{24,8},{1,17},{9,25},{17,1},{25,9},{2,18},{10... | collective-permute-start | bytes 983048 | tf_op jit(solution)/shard_map/ppermute | solution.py:31
  295.1 12.1 %collective-permute-start.8 = (bf16[6,1,2,1,1,1,2,16,512]{8,7,6,0,2,5,4,3,1:T(8,128)(2,1)S(1)}, bf16[6,1,2,1,1,1,2,16,512]{8,7,6,0,2,5,4,3,1:T(8,128)(2,1)S(1)}, u32[]{:S(2)}, u32[]{:S(2)}) collective-permute-start(bf16[6,1,2,1,1,1,2,16,512]{8,7,6,0,2,5,4,3,1:T(8,128)(2,1)S(1)} %constant_dynamic-slice_fusion.12), channel_id=1, source_target_pairs={{0,4},{4,0},{1,5},{5,1},{2,6},{6,2},{3,7},{7,3},{8,12},{12,8},{9,1... | collective-permute-start | bytes 1179656 | tf_op jit(solution)/shard_map/ppermute | solution.py:31
  297.3 15.7 %collective-permute-start.17 = (bf16[6,1,2,1,1,1,2,16,512]{8,7,6,0,2,5,4,3,1:T(8,128)(2,1)S(1)}, bf16[6,1,2,1,1,1,2,16,512]{8,7,6,0,2,5,4,3,1:T(8,128)(2,1)S(1)}, u32[]{:S(2)}, u32[]{:S(2)}) collective-permute-start(bf16[6,1,2,1,1,1,2,16,512]{8,7,6,0,2,5,4,3,1:T(8,128)(2,1)S(1)} %constant_dynamic-slice_fusion), channel_id=1, source_target_pairs={{0,4},{4,0},{1,5},{5,1},{2,6},{6,2},{3,7},{7,3},{8,12},{12,8},{9,1... | collective-permute-start | bytes 1179656 | tf_op jit(solution)/shard_map/ppermute | solution.py:31
  314.8 29.0 %all-to-all-start = ((bf16[2,16,2,1,2,16,512]{6,5,4,1,0,3,2:T(8,128)(2,1)}), bf16[2,16,2,1,2,16,512]{6,5,4,1,0,3,2:T(8,128)(2,1)}, u32[]{:S(2)}, u32[]{:S(2)}) async-start(bf16[2,16,2,1,2,16,512]{6,5,4,1,0,3,2:T(8,128)(2,1)} %maximum_bitcast_fusion), calls=%async_computation | async-start | bytes 4194304 | tf_op jit(solution)/shard_map/all_to_all | solution.py:41
  351.9 29.9 %all-to-all-start.3 = ((bf16[4,1,2,4,2,2,1,16,512]{8,0,5,4,3,2,6,1,7:T(4,128)(2,1)}), bf16[4,1,2,4,2,2,1,16,512]{8,0,5,4,3,2,6,1,7:T(4,128)(2,1)S(1)}, u32[]{:S(2)}, u32[]{:S(2)}) async-start(bf16[4,1,2,4,2,2,1,16,512]{8,0,5,4,3,2,6,1,7:T(4,128)(2,1)} %copy.72), calls=%async_computation.3 | async-start | bytes 4194304 | tf_op jit(solution)/shard_map/all_to_all | solution.py:79
  355.8 2.8 copy-start.1
  381.8 14.0 %slice-start.2 = ((s8[8388608]{0:T(1024)(128)(4,1)}), s8[4194304]{0:T(1024)(128)(4,1)S(1)}, s32[]{:S(2)}) async-start(s8[8388608]{0:T(1024)(128)(4,1)} %bitcast.117), calls=%async_computation.8 | async-start | bytes 8388608
  386.7 9.1 %slice-start = ((s8[8388608]{0:T(1024)(128)(4,1)}), s8[4194304]{0:T(1024)(128)(4,1)S(1)}, s32[]{:S(2)}) async-start(s8[8388608]{0:T(1024)(128)(4,1)} %bitcast.114), calls=%async_computation.6 | async-start | bytes 8388608
  386.8 9.1 %slice-start.3 = ((s8[8388608]{0:T(1024)(128)(4,1)}), s8[4194304]{0:T(1024)(128)(4,1)S(1)}, s32[]{:S(2)}) async-start(s8[8388608]{0:T(1024)(128)(4,1)} %bitcast.117), calls=%async_computation.9 | async-start | bytes 8388608
  389.2 6.6 %slice-start.1 = ((s8[8388608]{0:T(1024)(128)(4,1)}), s8[4194304]{0:T(1024)(128)(4,1)S(1)}, s32[]{:S(2)}) async-start(s8[8388608]{0:T(1024)(128)(4,1)} %bitcast.114), calls=%async_computation.7 | async-start | bytes 8388608
  395.9 13.4 %copy-start.2 = (bf16[8,512,512]{2,1,0:T(8,128)(2,1)S(1)}, bf16[8,512,512]{2,1,0:T(8,128)(2,1)}, u32[]{:S(2)}) copy-start(bf16[8,512,512]{2,1,0:T(8,128)(2,1)} %param.5) | copy-start | bytes 12582916
  423.0 6.6 %copy-start.3 = (f32[1,4,2,2,4,4,2,2,512]{8,5,7,6,4,3,2,1,0:T(4,128)S(1)}, f32[1,4,2,2,4,4,2,2,512]{8,5,7,6,4,3,2,1,0:T(4,128)}, u32[]{:S(2)}) copy-start(f32[1,4,2,2,4,4,2,2,512]{8,5,7,6,4,3,2,1,0:T(4,128)} %get-tuple-element.37) | copy-start | bytes 6291460
